TPU v7x, 32 devices: a whole 2x2x4 slice. The times are simulated.
32 devices in a mesh: lat: 4 (over y, x), lev: 8 (over z, core).
Axes of the slice: x: 2, y: 2, z: 4, core: 2. Of those that a mesh axis runs over, the one named last changes fastest.
Arguments:
- state: float32 [6, 12, 32, 1152], P(None, 'lat', 'lev'), may hold values from -6 to 6
- courant: float32 [2, 12, 32, 1152], P(None, 'lat', 'lev'), may hold values from -0.4 to 0.4
- offsets: int32 [2, 12, 32, 1152], P(None, 'lat', 'lev'), may hold values from -1 to 2
- log_thickness: float32 [12, 32, 1152], P('lat', 'lev'), may hold values from 0.05 to 0.5
- surface: float32 [12, 1152], P('lat'), may hold values from -6 to 6
- remap_level: int32 [12, 32, 1152], P('lat', None, 'lev'), may hold values from 0 to 31, as said below
- remap_weight: float32 [12, 32, 1152], P('lat', None, 'lev'), may hold values from 0 to 1
Outputs:
- remapped: float32 [6, 12, 32, 1152], P(None, 'lat', 'lev')
- geopotential: float32 [12, 32, 1152], P('lat', 'lev')
Inputs may be any that keep to these rules, and one draw needn't show every extreme that they name: `remap_level`: the source level of target level k lies within 2 of k.
All inputs are finite; a program needn't handle non-finite values.
Results may differ from a plain program's by a relative error of at most 0.00007.
Values sent between devices are 32-bit elements; how exact they have to be, the bound alone decides.
A program may use at most 64 MiB of HBM per device.

v0:
```python
import jax
import jax.numpy as jnp
from jax import lax
from jax.sharding import PartitionSpec as P

SUBSTEPS = 2


def extended_2(block, sides, width):
    for axis, dim in sides:
        count = lax.axis_size(axis)
        forward = [(i, i + 1) for i in range(count - 1)]
        backward = [(target, source) for source, target in forward]
        low = lax.ppermute(
            lax.slice_in_dim(block, block.shape[dim] - width, None, axis=dim), axis, forward
        )
        high = lax.ppermute(lax.slice_in_dim(block, 0, width, axis=dim), axis, backward)
        block = jnp.concatenate([low, block, high], axis=dim)
    return block


def from_behind(x, axis, by):
    count = lax.axis_size(axis)
    pairs = [(i, i + by) for i in range(count) if 0 <= i + by < count]
    return lax.ppermute(x, axis, pairs)


def entering(x, axis, combine, identity):
    count, position = (lax.axis_size(axis), lax.axis_index(axis))
    everything = lax.all_gather(x, axis)
    start = jnp.broadcast_to(jnp.asarray(identity, x.dtype), x.shape)

    def lap(k, before):
        at = count - 1 - k
        reached = at > position
        new = combine(before, everything[at])
        return jnp.where(reached, new, before)

    return lax.fori_loop(0, count, lap, start)


def local_parabola(extended, delta, weight):
    margin = 4
    count = extended.shape[-2] - 2 * margin
    edges = (
        7.0 * (extended[..., 1:-2, :] + extended[..., 2:-1, :])
        - (extended[..., :-3, :] + extended[..., 3:, :])
    ) / 12.0
    centre = jnp.zeros(extended.shape[:-2] + (count, extended.shape[-1]), jnp.float32)
    left = centre
    right = centre
    for offset in range(-2, 3):
        chosen = delta == offset
        start = margin + offset
        centre = jnp.where(chosen, extended[..., start : start + count, :], centre)
        left = jnp.where(chosen, edges[..., start - 2 : start - 2 + count, :], left)
        right = jnp.where(chosen, edges[..., start - 1 : start - 1 + count, :], right)
    slope = right - left
    curve = 6.0 * centre - 3.0 * (left + right)
    return left + weight * (slope + curve * (1.0 - weight))


def add_terms(earlier, later):
    return earlier + later


def per_device(state, courant, offsets, log_thickness, surface, remap_level, remap_weight):
    count, rows, levels, width = state.shape
    north_masks = [offsets[0] == offset for offset in range(-1, 3)]
    east_masks = [offsets[1] == offset for offset in range(-1, 3)]
    field = state
    for substep in range(SUBSTEPS):
        padded = extended_2(field, (("lat", 1),), 2)
        picked = jnp.zeros_like(field)
        for number, offset in enumerate(range(-1, 3)):
            picked = jnp.where(
                north_masks[number][None], padded[:, offset + 2 : offset + 2 + rows], picked
            )
        north = courant[0][None] * picked
        below = from_behind(north[:, rows - 1 :], "lat", 1)
        south = jnp.concatenate([below, north[:, : rows - 1]], axis=1)
        moved = jnp.zeros_like(field)
        for number, offset in enumerate(range(-1, 3)):
            moved = jnp.where(east_masks[number][None], jnp.roll(field, -offset, axis=3), moved)
        east = courant[1][None] * moved
        west = jnp.roll(east, 1, axis=3)
        field = field - (north - south) - (east - west)
    heating = field[0] * log_thickness
    lower_local = jnp.cumsum(heating[:, ::-1], axis=1)[:, ::-1] - heating
    column_sum = jnp.sum(heating, axis=1)
    deeper = entering(column_sum, "lev", add_terms, jnp.zeros_like(column_sum))
    geopotential = surface[:, None, :] + deeper[:, None, :] + lower_local + 0.5 * heating
    total_levels = remap_level.shape[1]
    delta_col = (remap_level - jnp.arange(total_levels, dtype=jnp.int32)[None, :, None]).astype(
        jnp.float32
    )
    inputs = lax.all_to_all(
        jnp.stack([delta_col, remap_weight]), "lev", split_axis=2, concat_axis=3, tiled=True
    )
    margin = 4
    before = []
    before.insert(0, from_behind(field, "lev", 1))
    after_list = [from_behind(field, "lev", -1)]
    joined = jnp.concatenate(before + [field] + after_list, axis=2)
    first = lax.axis_index("lev") * levels
    whole = levels * lax.axis_size("lev")
    position = first - margin + jnp.arange(levels + 2 * margin, dtype=jnp.int32)
    where_from = jnp.clip(position, 0, whole - 1) - (first - margin)
    extended = jnp.take(joined, where_from, axis=2)
    remapped = local_parabola(extended, inputs[0][None], inputs[1][None])
    return (remapped, geopotential)


def solution(mesh):
    in_specs = (
        P(None, "lat", "lev", None),
        P(None, "lat", "lev", None),
        P(None, "lat", "lev", None),
        P("lat", "lev", None),
        P("lat", None),
        P("lat", None, "lev"),
        P("lat", None, "lev"),
    )
    out_specs = (P(None, "lat", "lev", None), P("lat", "lev", None))
    return jax.shard_map(
        per_device, mesh=mesh, in_specs=in_specs, out_specs=out_specs, check_vma=False
    )
```

profile of v0, /device:TPU:5, one launch (start us, length us, event | category | flops | bytes accessed | tf_op | source)
XLA Modules:
  0.0 88.0 jit_solution(11633455858299982283)
XLA Ops:
  0.6 1.1 %copy.167 = f32[6,3,4,1152]{3,0,1,2:T(8,128)S(1)} copy(f32[6,3,4,1152]{3,2,1,0:T(4,128)} %param.9) | data formatting | bytes 663552 | tf_op args[0]
  1.7 0.8 fusion.43
  2.6 3.1 %collective-permute-start = (f32[6,2,4,1152]{3,0,1,2:T(8,128)}, f32[6,2,4,1152]{3,0,1,2:T(8,128)}, u32[]{:S(2)}, u32[]{:S(2)}) collective-permute-start(f32[6,2,4,1152]{3,0,1,2:T(8,128)} %get-tuple-element.158), channel_id=1, source_target_pairs={{8,0},{16,8},{24,16},{9,1},{17,9},{25,17},{10,2},{18,10},{26,18},{... | collective-permute-start | bytes 663560 | tf_op jit(solution)/shard_map/ppermute | solution.py:17
  5.6 2.9 %collective-permute-start.1 = (f32[6,2,4,1152]{3,0,1,2:T(8,128)}, f32[6,2,4,1152]{3,0,1,2:T(8,128)}, u32[]{:S(2)}, u32[]{:S(2)}) collective-permute-start(f32[6,2,4,1152]{3,0,1,2:T(8,128)} %get-tuple-element.159), channel_id=1, source_target_pairs={{0,8},{8,16},{16,24},{1,9},{9,17},{17,25},{2,10},{10,18},{18,26},{... | collective-permute-start | bytes 663560 | tf_op jit(solution)/shard_map/ppermute | solution.py:14
  8.6 0.8 copy.154
  9.5 6.1 %all-to-all-start = ((f32[2,3,32,144]{3,0,1,2:T(2,128)}), f32[2,3,32,144]{3,0,1,2:T(2,128)S(1)}, u32[]{:S(2)}, u32[]{:S(2)}) async-start(f32[2,3,32,144]{3,0,1,2:T(2,128)} %copy.154), calls=%async_computation | async-start | bytes 393216 | tf_op jit(solution)/shard_map/all_to_all | solution.py:97
  15.8 0.7 fusion.41
  16.5 0.2 slice.243
  16.6 0.6 slice.244
  17.6 0.6 copy.158
  18.2 0.6 copy.161
  18.9 0.6 copy.162
  19.5 0.6 copy.163
  20.1 0.6 copy.157
  20.8 1.2 %fusion.30 = (f32[6,3,4,1152]{3,0,1,2:T(8,128)S(1)}, f32[6,5,4,1152]{3,0,1,2:T(8,128)S(1)}) fusion(f32[6,3,4,2]{3,0,1,2:T(8,128)} %slice.244, f32[6,3,4,1150]{3,0,1,2:T(8,128)S(1)} %slice.243, f32[6,3,4,1]{3,0,1,2:T(8,128)} %get-tuple-element.155, f32[6,3,4,1151]{3,0,1,2:T(8,128)S(1)} %get-tuple-element.157, f32[6,3,4,1151]{3,0,1,2:T(8,128)S(1)} %get-tuple-element.156, ...), kind=kLoop, calls=%fused_computation.46 | loop fusion | flops 663551 | bytes 2322432 | tf_op jit(solution)/shard_map/mul | solution.py:85
  22.2 0.6 compare_and_fusion
  23.0 1.0 %constant_dynamic-update-slice_fusion = f32[6,5,4,1152]{3,0,1,2:T(8,128)S(1)} fusion(f32[6,5,4,1152]{3,0,1,2:T(8,128)S(1)} %get-tuple-element.161, f32[6,2,4,1152]{3,0,1,2:T(8,128)} %collective-permute-done), kind=kLoop, calls=%fused_computation.83 | loop fusion | bytes 516096 | tf_op jit(solution)/shard_map/concatenate | solution.py:18
  24.1 1.2 %fusion.27 = f32[6,3,4,1152]{3,0,1,2:T(8,128)S(1)} fusion(f32[6,3,4,1152]{3,0,1,2:T(8,128)S(1)} %copy.167, f32[6,2,4,1152]{3,0,1,2:T(8,128)} %collective-permute-done.1, f32[6,5,4,1152]{3,0,1,2:T(8,128)S(1)} %constant_dynamic-update-slice_fusion, f32[3,4,1152]{2,0,1:T(4,128)S(1)} %copy-done.1, pred[3,4,1152]{2,0,1:T(4,128)(4,1)S(1)} %copy-done.17, ...), kind=kLoop, calls=%fused_computation.41 | loop fusion | flops 497664 | bytes 1658880 | tf_op jit(solution)/shard_map/mul | solution.py:79
  25.3 1.9 %collective-permute-start.2 = (f32[6,1,4,1152]{3,0,1,2:T(8,128)S(1)}, f32[6,1,4,1152]{3,0,1,2:T(8,128)S(1)}, u32[]{:S(2)}, u32[]{:S(2)}) collective-permute-start(f32[6,1,4,1152]{3,0,1,2:T(8,128)S(1)} %slice.241), channel_id=1, source_target_pairs={{0,8},{8,16},{16,24},{1,9},{9,17},{17,25},{2,10},{10,18},{18,26},{... | collective-permute-start | bytes 331784 | tf_op jit(solution)/shard_map/ppermute | solution.py:25
  27.4 0.6 copy.156
  28.2 0.6 copy.181
  28.9 0.6 copy.182
  29.7 0.6 copy.183
  30.4 0.6 copy.184
  31.1 1.3 %collective-permute-done.2 = f32[6,1,4,1152]{3,0,1,2:T(8,128)S(1)} collective-permute-done((f32[6,1,4,1152]{3,0,1,2:T(8,128)S(1)}, f32[6,1,4,1152]{3,0,1,2:T(8,128)S(1)}, u32[]{:S(2)}, u32[]{:S(2)}) %collective-permute-start.2) | collective-permute-done | bytes 110624 | tf_op jit(solution)/shard_map/ppermute | solution.py:25
  32.4 0.2 fusion.29
  32.6 0.2 fusion.39
  32.8 0.2 slice.257
  33.1 3.2 %collective-permute-start.3 = (f32[6,2,4,1152]{3,0,1,2:T(8,128)S(1)}, f32[6,2,4,1152]{3,0,1,2:T(8,128)S(1)}, u32[]{:S(2)}, u32[]{:S(2)}) collective-permute-start(f32[6,2,4,1152]{3,0,1,2:T(8,128)S(1)} %get-tuple-element.153), channel_id=1, source_target_pairs={{8,0},{16,8},{24,16},{9,1},{17,9},{25,17},{10,2},{18,10},{26,18},{... | collective-permute-start | bytes 663560 | tf_op jit(solution)/shard_map/ppermute | solution.py:17
  36.2 2.3 %collective-permute-start.4 = (f32[6,2,4,1152]{3,0,1,2:T(8,128)S(1)}, f32[6,2,4,1152]{3,0,1,2:T(8,128)S(1)}, u32[]{:S(2)}, u32[]{:S(2)}) collective-permute-start(f32[6,2,4,1152]{3,0,1,2:T(8,128)S(1)} %get-tuple-element.152), channel_id=1, source_target_pairs={{0,8},{8,16},{16,24},{1,9},{9,17},{17,25},{2,10},{10,18},{18,26},{... | collective-permute-start | bytes 663560 | tf_op jit(solution)/shard_map/ppermute | solution.py:14
  38.6 3.1 %collective-permute-done.3 = f32[6,2,4,1152]{3,0,1,2:T(8,128)S(1)} collective-permute-done((f32[6,2,4,1152]{3,0,1,2:T(8,128)S(1)}, f32[6,2,4,1152]{3,0,1,2:T(8,128)S(1)}, u32[]{:S(2)}, u32[]{:S(2)}) %collective-permute-start.3) | collective-permute-done | bytes 221216 | tf_op jit(solution)/shard_map/ppermute | solution.py:17
  41.7 7.0 %collective-permute-done.4 = f32[6,2,4,1152]{3,0,1,2:T(8,128)S(1)} collective-permute-done((f32[6,2,4,1152]{3,0,1,2:T(8,128)S(1)}, f32[6,2,4,1152]{3,0,1,2:T(8,128)S(1)}, u32[]{:S(2)}, u32[]{:S(2)}) %collective-permute-start.4) | collective-permute-done | bytes 221216 | tf_op jit(solution)/shard_map/ppermute | solution.py:14
  48.7 0.3 fusion.5
  49.0 2.9 %collective-permute-start.5 = (f32[6,1,4,1152]{3,0,1,2:T(8,128)S(1)}, f32[6,1,4,1152]{3,0,1,2:T(8,128)S(1)}, u32[]{:S(2)}, u32[]{:S(2)}) collective-permute-start(f32[6,1,4,1152]{3,0,1,2:T(8,128)S(1)} %slice.255), channel_id=1, source_target_pairs={{0,8},{8,16},{16,24},{1,9},{9,17},{17,25},{2,10},{10,18},{18,26},{... | collective-permute-start | bytes 331784 | tf_op jit(solution)/shard_map/ppermute | solution.py:25
  52.0 0.4 fusion.34
  52.5 3.3 %collective-permute-done.5 = f32[6,1,4,1152]{3,0,1,2:T(8,128)S(1)} collective-permute-done((f32[6,1,4,1152]{3,0,1,2:T(8,128)S(1)}, f32[6,1,4,1152]{3,0,1,2:T(8,128)S(1)}, u32[]{:S(2)}, u32[]{:S(2)}) %collective-permute-start.5) | collective-permute-done | bytes 110624 | tf_op jit(solution)/shard_map/ppermute | solution.py:25
  55.8 0.2 fusion.33
  56.0 6.5 %collective-permute-start.6 = (f32[6,3,4,1152]{3,0,1,2:T(8,128)S(1)}, f32[6,3,4,1152]{3,0,1,2:T(8,128)S(1)}, u32[]{:S(2)}, u32[]{:S(2)}) collective-permute-start(f32[6,3,4,1152]{3,0,1,2:T(8,128)S(1)} %fusion.33), channel_id=1, source_target_pairs={{0,1},{1,2},{2,3},{3,4},{4,5},{5,6},{6,7},{8,9},{9,10},{10,11},{11... | collective-permute-start | bytes 995336 | tf_op jit(solution)/shard_map/ppermute | solution.py:25
  62.6 1.9 %collective-permute-start.7 = (f32[6,3,4,1152]{3,0,1,2:T(8,128)S(1)}, f32[6,3,4,1152]{3,0,1,2:T(8,128)S(1)}, u32[]{:S(2)}, u32[]{:S(2)}) collective-permute-start(f32[6,3,4,1152]{3,0,1,2:T(8,128)S(1)} %fusion.33), channel_id=1, source_target_pairs={{1,0},{2,1},{3,2},{4,3},{5,4},{6,5},{7,6},{9,8},{10,9},{11,10},{12... | collective-permute-start | bytes 995336 | tf_op jit(solution)/shard_map/ppermute | solution.py:25
  64.6 18.3 %all-gather.1 = f32[8,3,1152]{2,1,0:T(4,128)S(1)} all-gather(f32[1,3,1152]{2,1,0:T(4,128)S(1)} %bitcast.59), channel_id=2, replica_groups=mesh['lat'=4,'lev'=8] {'lev'}, dimensions={0}, use_global_device_ids=true | all-gather | bytes 124416 | tf_op jit(solution)/shard_map/all_gather | solution.py:30
  82.9 0.4 while.16
  83.3 0.3 rev.6
  83.7 0.3 rev.7
  84.1 0.6 multiply_add_fusion
  85.0 0.6 gather_fusion
  86.0 0.5 copy-done.23
  86.6 0.5 fusion.15
  87.2 0.8 copy.188
  (116 shorter events, 2.9 us)
Async XLA Ops:
  0.6 7.9 %copy-start.21 = (s32[3,32,144]{2,1,0:T(8,128)S(1)}, s32[3,32,144]{2,1,0:T(8,128)}, u32[]{:S(2)}) copy-start(s32[3,32,144]{2,1,0:T(8,128)} %param.14) | copy-start | bytes 165892
  0.6 8.0 %copy-start.22 = (f32[3,32,144]{2,1,0:T(8,128)S(1)}, f32[3,32,144]{2,1,0:T(8,128)}, u32[]{:S(2)}) copy-start(f32[3,32,144]{2,1,0:T(8,128)} %param.15) | copy-start | bytes 165892
  2.6 20.4 %collective-permute-start = (f32[6,2,4,1152]{3,0,1,2:T(8,128)}, f32[6,2,4,1152]{3,0,1,2:T(8,128)}, u32[]{:S(2)}, u32[]{:S(2)}) collective-permute-start(f32[6,2,4,1152]{3,0,1,2:T(8,128)} %get-tuple-element.158), channel_id=1, source_target_pairs={{8,0},{16,8},{24,16},{9,1},{17,9},{25,17},{10,2},{18,10},{26,18},{... | collective-permute-start | bytes 663560 | tf_op jit(solution)/shard_map/ppermute | solution.py:17
  5.6 18.4 %collective-permute-start.1 = (f32[6,2,4,1152]{3,0,1,2:T(8,128)}, f32[6,2,4,1152]{3,0,1,2:T(8,128)}, u32[]{:S(2)}, u32[]{:S(2)}) collective-permute-start(f32[6,2,4,1152]{3,0,1,2:T(8,128)} %get-tuple-element.159), channel_id=1, source_target_pairs={{0,8},{8,16},{16,24},{1,9},{9,17},{17,25},{2,10},{10,18},{18,26},{... | collective-permute-start | bytes 663560 | tf_op jit(solution)/shard_map/ppermute | solution.py:14
  9.5 13.3 %all-to-all-start = ((f32[2,3,32,144]{3,0,1,2:T(2,128)}), f32[2,3,32,144]{3,0,1,2:T(2,128)S(1)}, u32[]{:S(2)}, u32[]{:S(2)}) async-start(f32[2,3,32,144]{3,0,1,2:T(2,128)} %copy.154), calls=%async_computation | async-start | bytes 393216 | tf_op jit(solution)/shard_map/all_to_all | solution.py:97
  15.6 1.7 %copy-start.19 = (s32[2,3,4,1152]{3,2,1,0:T(4,128)S(1)}, s32[2,3,4,1152]{3,2,1,0:T(4,128)}, u32[]{:S(2)}) copy-start(s32[2,3,4,1152]{3,2,1,0:T(4,128)} %param.11) | copy-start | bytes 331780
  15.6 2.0 %copy-start.20 = (f32[2,3,4,1152]{3,2,1,0:T(4,128)S(1)}, f32[2,3,4,1152]{3,2,1,0:T(4,128)}, u32[]{:S(2)}) copy-start(f32[2,3,4,1152]{3,2,1,0:T(4,128)} %param.10) | copy-start | bytes 331780
  15.8 5.0 %copy-start = (f32[6,3,4,1152]{3,2,1,0:T(4,128)S(1)}, f32[6,3,4,1152]{3,2,1,0:T(4,128)}, u32[]{:S(2)}) copy-start(f32[6,3,4,1152]{3,2,1,0:T(4,128)} %param.9) | copy-start | bytes 995332
  17.4 4.5 %copy-start.3 = (pred[3,4,1152]{2,0,1:T(4,128)(4,1)}, pred[3,4,1152]{2,0,1:T(4,128)(4,1)S(1)}, u32[]{:S(2)}) copy-start(pred[3,4,1152]{2,0,1:T(4,128)(4,1)S(1)} %copy.169) | copy-start | bytes 41476
  17.5 4.5 %copy-start.5 = (pred[3,4,1152]{2,0,1:T(4,128)(4,1)}, pred[3,4,1152]{2,0,1:T(4,128)(4,1)S(1)}, u32[]{:S(2)}) copy-start(pred[3,4,1152]{2,0,1:T(4,128)(4,1)S(1)} %copy.172) | copy-start | bytes 41476
  17.5 4.5 %copy-start.7 = (pred[3,4,1152]{2,0,1:T(4,128)(4,1)}, pred[3,4,1152]{2,0,1:T(4,128)(4,1)S(1)}, u32[]{:S(2)}) copy-start(pred[3,4,1152]{2,0,1:T(4,128)(4,1)S(1)} %copy.175) | copy-start | bytes 41476
  17.6 4.4 %copy-start.9 = (pred[3,4,1152]{2,0,1:T(4,128)(4,1)}, pred[3,4,1152]{2,0,1:T(4,128)(4,1)S(1)}, u32[]{:S(2)}) copy-start(pred[3,4,1152]{2,0,1:T(4,128)(4,1)S(1)} %copy.176) | copy-start | bytes 41476
  22.0 2.0 %copy-start.1 = (f32[3,4,1152]{2,0,1:T(4,128)S(1)}, f32[3,4,1152]{2,0,1:T(4,128)}, u32[]{:S(2)}) copy-start(f32[3,4,1152]{2,0,1:T(4,128)} %copy.157) | copy-start | bytes 165892
  22.0 2.0 %copy-start.11 = (pred[3,4,1152]{2,0,1:T(4,128)(4,1)S(1)}, pred[3,4,1152]{2,0,1:T(4,128)(4,1)}, u32[]{:S(2)}) copy-start(pred[3,4,1152]{2,0,1:T(4,128)(4,1)} %copy.158) | copy-start | bytes 41476
  22.0 2.0 %copy-start.13 = (pred[3,4,1152]{2,0,1:T(4,128)(4,1)S(1)}, pred[3,4,1152]{2,0,1:T(4,128)(4,1)}, u32[]{:S(2)}) copy-start(pred[3,4,1152]{2,0,1:T(4,128)(4,1)} %copy.161) | copy-start | bytes 41476
  22.1 2.0 %copy-start.15 = (pred[3,4,1152]{2,0,1:T(4,128)(4,1)S(1)}, pred[3,4,1152]{2,0,1:T(4,128)(4,1)}, u32[]{:S(2)}) copy-start(pred[3,4,1152]{2,0,1:T(4,128)(4,1)} %copy.162) | copy-start | bytes 41476
  22.1 2.0 %copy-start.17 = (pred[3,4,1152]{2,0,1:T(4,128)(4,1)S(1)}, pred[3,4,1152]{2,0,1:T(4,128)(4,1)}, u32[]{:S(2)}) copy-start(pred[3,4,1152]{2,0,1:T(4,128)(4,1)} %copy.163) | copy-start | bytes 41476
  25.3 7.1 %collective-permute-start.2 = (f32[6,1,4,1152]{3,0,1,2:T(8,128)S(1)}, f32[6,1,4,1152]{3,0,1,2:T(8,128)S(1)}, u32[]{:S(2)}, u32[]{:S(2)}) collective-permute-start(f32[6,1,4,1152]{3,0,1,2:T(8,128)S(1)} %slice.241), channel_id=1, source_target_pairs={{0,8},{8,16},{16,24},{1,9},{9,17},{17,25},{2,10},{10,18},{18,26},{... | collective-permute-start | bytes 331784 | tf_op jit(solution)/shard_map/ppermute | solution.py:25
  32.7 15.9 %copy-start.12 = (pred[3,4,1152]{2,0,1:T(4,128)(4,1)S(1)}, pred[3,4,1152]{2,0,1:T(4,128)(4,1)}, u32[]{:S(2)}) copy-start(pred[3,4,1152]{2,0,1:T(4,128)(4,1)} %copy.158) | copy-start | bytes 41476
  32.7 15.9 %copy-start.14 = (pred[3,4,1152]{2,0,1:T(4,128)(4,1)S(1)}, pred[3,4,1152]{2,0,1:T(4,128)(4,1)}, u32[]{:S(2)}) copy-start(pred[3,4,1152]{2,0,1:T(4,128)(4,1)} %copy.161) | copy-start | bytes 41476
  32.8 15.9 %copy-start.16 = (pred[3,4,1152]{2,0,1:T(4,128)(4,1)S(1)}, pred[3,4,1152]{2,0,1:T(4,128)(4,1)}, u32[]{:S(2)}) copy-start(pred[3,4,1152]{2,0,1:T(4,128)(4,1)} %copy.162) | copy-start | bytes 41476
  32.8 15.9 %copy-start.18 = (pred[3,4,1152]{2,0,1:T(4,128)(4,1)S(1)}, pred[3,4,1152]{2,0,1:T(4,128)(4,1)}, u32[]{:S(2)}) copy-start(pred[3,4,1152]{2,0,1:T(4,128)(4,1)} %copy.163) | copy-start | bytes 41476
  33.0 18.9 %copy-start.4 = (pred[3,4,1152]{2,0,1:T(4,128)(4,1)S(1)}, pred[3,4,1152]{2,0,1:T(4,128)(4,1)}, u32[]{:S(2)}) copy-start(pred[3,4,1152]{2,0,1:T(4,128)(4,1)} %copy-done.3) | copy-start | bytes 41476
  33.0 18.9 %copy-start.6 = (pred[3,4,1152]{2,0,1:T(4,128)(4,1)S(1)}, pred[3,4,1152]{2,0,1:T(4,128)(4,1)}, u32[]{:S(2)}) copy-start(pred[3,4,1152]{2,0,1:T(4,128)(4,1)} %copy-done.5) | copy-start | bytes 41476
  33.0 18.9 %copy-start.8 = (pred[3,4,1152]{2,0,1:T(4,128)(4,1)S(1)}, pred[3,4,1152]{2,0,1:T(4,128)(4,1)}, u32[]{:S(2)}) copy-start(pred[3,4,1152]{2,0,1:T(4,128)(4,1)} %copy-done.7) | copy-start | bytes 41476
  33.0 18.9 %copy-start.10 = (pred[3,4,1152]{2,0,1:T(4,128)(4,1)S(1)}, pred[3,4,1152]{2,0,1:T(4,128)(4,1)}, u32[]{:S(2)}) copy-start(pred[3,4,1152]{2,0,1:T(4,128)(4,1)} %copy-done.9) | copy-start | bytes 41476
  33.1 8.6 %collective-permute-start.3 = (f32[6,2,4,1152]{3,0,1,2:T(8,128)S(1)}, f32[6,2,4,1152]{3,0,1,2:T(8,128)S(1)}, u32[]{:S(2)}, u32[]{:S(2)}) collective-permute-start(f32[6,2,4,1152]{3,0,1,2:T(8,128)S(1)} %get-tuple-element.153), channel_id=1, source_target_pairs={{8,0},{16,8},{24,16},{9,1},{17,9},{25,17},{10,2},{18,10},{26,18},{... | collective-permute-start | bytes 663560 | tf_op jit(solution)/shard_map/ppermute | solution.py:17
  36.2 12.5 %collective-permute-start.4 = (f32[6,2,4,1152]{3,0,1,2:T(8,128)S(1)}, f32[6,2,4,1152]{3,0,1,2:T(8,128)S(1)}, u32[]{:S(2)}, u32[]{:S(2)}) collective-permute-start(f32[6,2,4,1152]{3,0,1,2:T(8,128)S(1)} %get-tuple-element.152), channel_id=1, source_target_pairs={{0,8},{8,16},{16,24},{1,9},{9,17},{17,25},{2,10},{10,18},{18,26},{... | collective-permute-start | bytes 663560 | tf_op jit(solution)/shard_map/ppermute | solution.py:14
  49.0 6.8 %collective-permute-start.5 = (f32[6,1,4,1152]{3,0,1,2:T(8,128)S(1)}, f32[6,1,4,1152]{3,0,1,2:T(8,128)S(1)}, u32[]{:S(2)}, u32[]{:S(2)}) collective-permute-start(f32[6,1,4,1152]{3,0,1,2:T(8,128)S(1)} %slice.255), channel_id=1, source_target_pairs={{0,8},{8,16},{16,24},{1,9},{9,17},{17,25},{2,10},{10,18},{18,26},{... | collective-permute-start | bytes 331784 | tf_op jit(solution)/shard_map/ppermute | solution.py:25
  55.8 8.7 %copy-start.28 = (f32[3,4,1152]{2,1,0:T(4,128)S(1)}, f32[3,4,1152]{2,1,0:T(4,128)}, u32[]{:S(2)}) copy-start(f32[3,4,1152]{2,1,0:T(4,128)} %param.12) | copy-start | bytes 165892
  55.8 27.1 %copy-start.2 = (f32[3,1152]{1,0:T(4,128)S(1)}, f32[3,1152]{1,0:T(4,128)}, u32[]{:S(2)}) copy-start(f32[3,1152]{1,0:T(4,128)} %custom-call) | copy-start | bytes 41476
  55.8 28.3 %copy-start.29 = (f32[3,1152]{1,0:T(4,128)S(1)}, f32[3,1152]{1,0:T(4,128)}, u32[]{:S(2)}) copy-start(f32[3,1152]{1,0:T(4,128)} %param.13) | copy-start | bytes 41476
  56.0 28.7 %collective-permute-start.6 = (f32[6,3,4,1152]{3,0,1,2:T(8,128)S(1)}, f32[6,3,4,1152]{3,0,1,2:T(8,128)S(1)}, u32[]{:S(2)}, u32[]{:S(2)}) collective-permute-start(f32[6,3,4,1152]{3,0,1,2:T(8,128)S(1)} %fusion.33), channel_id=1, source_target_pairs={{0,1},{1,2},{2,3},{3,4},{4,5},{5,6},{6,7},{8,9},{9,10},{10,11},{11... | collective-permute-start | bytes 995336 | tf_op jit(solution)/shard_map/ppermute | solution.py:25
  62.6 22.1 %collective-permute-start.7 = (f32[6,3,4,1152]{3,0,1,2:T(8,128)S(1)}, f32[6,3,4,1152]{3,0,1,2:T(8,128)S(1)}, u32[]{:S(2)}, u32[]{:S(2)}) collective-permute-start(f32[6,3,4,1152]{3,0,1,2:T(8,128)S(1)} %fusion.33), channel_id=1, source_target_pairs={{1,0},{2,1},{3,2},{4,3},{5,4},{6,5},{7,6},{9,8},{10,9},{11,10},{12... | collective-permute-start | bytes 995336 | tf_op jit(solution)/shard_map/ppermute | solution.py:25
  85.0 0.7 copy-start.30
  85.8 0.7 copy-start.23
  85.8 0.7 copy-start.24
  85.8 0.7 copy-start.25
  85.8 0.7 copy-start.26
  85.9 0.8 copy-start.27
where the time goes:
time: 88.6 us; the launch traced here: 88 us
  starting transfers between devices  30.8 us (35%)
  blocking collectives  18.3 us (21%)
  local copies, waits for them, and re-layouts  16.3 us (18%)
  waiting for transfers between devices  14.7 us (17%)
  other arithmetic  6.29 us (7%)
  between operations  1.36 us (2%)
    all_gather x1, blocking collectives, entering(): everything = lax.all_gather(x, axis)  18.3 us
    ppermute x4, starting transfers between devices, from_behind(): return lax.ppermute(x, axis, pairs)  13.3 us
    ppermute x2, waiting for transfers between devices, extended_2(): lax.ppermute(lax.slice_in_dim(block, block.shape[dim] - width, None, axis...  7 us
    ppermute x2, starting transfers between devices, extended_2(): lax.ppermute(lax.slice_in_dim(block, 0, width, axis=dim), axis, backward)  6.2 us
    all_to_all x1, starting transfers between devices, per_device(): lax.all_to_all(jnp.stack([delta_col, remap_weight]), 'lev', split_axis=2,...  6.11 us
    ppermute x2, starting transfers between devices, extended_2(): lax.ppermute(lax.slice_in_dim(block, block.shape[dim] - width, None, axis...  5.2 us
    ppermute x4, waiting for transfers between devices, from_behind(): return lax.ppermute(x, axis, pairs)  4.58 us
    eq x10, local copies, waits for them, and re-layouts, local_parabola(): chosen = delta == offset  3.74 us
  transfers between devices with their start and end apart: 9, of which 4 were waited for; matrix products, arithmetic and copies ran while one was open for 17% of the time, Pallas kernels for 0%

commit v1 on v0

--- a/solution.py
+++ b/solution.py
@@ -1,6 +1,10 @@
+import functools
+
 import jax
 import jax.numpy as jnp
 from jax import lax
+from jax.experimental import pallas as pl
+from jax.experimental.pallas import tpu as pltpu
 from jax.sharding import PartitionSpec as P
 
 SUBSTEPS = 2
@@ -111,6 +115,370 @@
     return (remapped, geopotential)
 
 
+MARGIN = 4
+MESH = pl.DeviceIdType.MESH
+
+
+def remote(src, dst, send, recv, axis, peer):
+    return pltpu.make_async_remote_copy(
+        src_ref=src,
+        dst_ref=dst,
+        send_sem=send,
+        recv_sem=recv,
+        device_id={axis: peer},
+        device_id_type=MESH,
+    )
+
+
+def kernel(
+    lats,
+    levs,
+    chunks,
+    state,
+    courant,
+    offsets,
+    thickness,
+    surface,
+    remap_level,
+    remap_weight,
+    out,
+    geo,
+    pack,
+    pack_off,
+    work,
+    work_off,
+    mid,
+    ret,
+    ext,
+    rpack,
+    rrecv,
+    rall,
+    hsum,
+    sums,
+    deep,
+    fs,
+    fr,
+    gs,
+    gr,
+    bs,
+    br,
+    zs,
+    zr,
+    rs,
+    rr,
+    ss,
+    sr,
+):
+    count, rows, levels, width = state.shape
+    slab = rows * lats
+    piece = remap_level.shape[2]
+    span = width // chunks
+    me = lax.axis_index("lat")
+    lev = lax.axis_index("lev")
+
+    barrier = pltpu.get_barrier_semaphore()
+    for d in range(1, lats):
+        pl.semaphore_signal(
+            barrier, inc=1, device_id={"lat": lax.rem(me + d, lats)}, device_id_type=MESH
+        )
+    for d in range(1, levs):
+        pl.semaphore_signal(
+            barrier, inc=1, device_id={"lev": lax.rem(lev + d, levs)}, device_id_type=MESH
+        )
+
+    def pack_level(level):
+        at = pl.ds(level, 1)
+        for r in range(rows):
+            for f in range(count):
+                pack[level, r, f : f + 1, :] = state[f, r, at, :]
+            for f in range(2):
+                pack[level, r, count + f : count + f + 1, :] = courant[f, r, at, :]
+                pack_off[level, r, f : f + 1, :] = offsets[f, r, at, :]
+
+    fwd = []
+    for d in range(1, lats):
+        peer = lax.rem(me + d, lats)
+        pack_level(peer)
+        if d == 1:
+            pl.semaphore_wait(barrier, lats + levs - 2)
+        a = remote(
+            pack.at[peer], work.at[pl.ds(2 + rows * me, rows)], fs.at[d], fr.at[d], "lat", peer
+        )
+        b = remote(
+            pack_off.at[peer], work_off.at[pl.ds(1 + rows * me, rows)], gs.at[d], gr.at[d], "lat", peer
+        )
+        a.start()
+        b.start()
+        fwd += [a, b]
+
+    first = []
+    for p in range(levs):
+        for r in range(rows):
+            lo = p * levels
+            ks = lo + lax.broadcasted_iota(jnp.int32, (levels, piece), 0)
+            rpack[p, 0, r] = (remap_level[r, lo : lo + levels, :] - ks).astype(jnp.float32)
+            rpack[p, 1, r] = remap_weight[r, lo : lo + levels, :]
+    for d in range(1, levs):
+        peer = lax.rem(lev + d, levs)
+        c = remote(rpack.at[peer], rrecv.at[lev], rs.at[d], rr.at[d], "lev", peer)
+        c.start()
+        first.append(c)
+    rrecv[lev] = rpack[lev]
+
+    pack_level(me)
+    for r in range(rows):
+        work[2 + rows * me + r] = pack[me, r]
+        work_off[1 + rows * me + r] = pack_off[me, r]
+    blank = jnp.zeros(work.shape[1:], jnp.float32)
+    for r in (0, 1, slab + 2, slab + 3):
+        work[r] = blank
+        mid[r] = blank
+
+    for c in fwd:
+        c.wait_recv()
+
+    whole = work.shape[1:]
+
+    def substep(source, store):
+        def face(j, south):
+            q = source[j + 2]
+            o0 = jnp.broadcast_to(work_off[j + 1, 0:1, :], whole)
+            o1 = jnp.broadcast_to(work_off[j + 1, 1:2, :], whole)
+            c0 = jnp.broadcast_to(work[j + 2, count : count + 1, :], whole)
+            c1 = jnp.broadcast_to(work[j + 2, count + 1 : count + 2, :], whole)
+            up = jnp.where(
+                o0 <= 0,
+                jnp.where(o0 == 0, q, source[j + 1]),
+                jnp.where(o0 == 1, source[j + 3], source[j + 4]),
+            )
+            north = c0 * up
+            side = jnp.where(
+                o1 <= 0,
+                jnp.where(o1 == 0, q, pltpu.roll(q, 1, 1)),
+                jnp.where(o1 == 1, pltpu.roll(q, width - 1, 1), pltpu.roll(q, width - 2, 1)),
+            )
+            east = c1 * side
+            west = pltpu.roll(east, 1, 1)
+            store(j, q - (north - south) - (east - west))
+            return north
+
+        lax.fori_loop(0, slab, face, jnp.zeros(whole, jnp.float32))
+
+    def store_mid(j, value):
+        mid[j + 2] = value
+
+    def store_ret(j, value):
+        ret[j] = value[:count]
+
+    substep(work, store_mid)
+    substep(mid, store_ret)
+
+    back = []
+    for n in range(chunks):
+        lanes = pl.ds(n * span, span)
+        some = []
+        for d in range(1, lats):
+            peer = lax.rem(me + d, lats)
+            c = remote(
+                ret.at[pl.ds(rows * peer, rows), :, lanes],
+                ext.at[MARGIN + me, :, :, lanes],
+                bs.at[n, d],
+                br.at[n, d],
+                "lat",
+                peer,
+            )
+            c.start()
+            some.append(c)
+        back.append(some)
+    for r in range(rows):
+        ext[MARGIN + me, r] = ret[rows * me + r]
+    for c in first:
+        c.wait_recv()
+    for p in range(levs):
+        rall[:, :, :, p * piece : (p + 1) * piece] = rrecv[p]
+
+    def up_copy(n):
+        lanes = pl.ds(n * span, span)
+        return remote(
+            ext.at[pl.ds(levels, MARGIN), :, :, lanes],
+            ext.at[pl.ds(0, MARGIN), :, :, lanes],
+            zs.at[n, 0],
+            zr.at[n, 0],
+            "lev",
+            jnp.minimum(lev + 1, levs - 1),
+        )
+
+    def down_copy(n):
+        lanes = pl.ds(n * span, span)
+        return remote(
+            ext.at[pl.ds(MARGIN, MARGIN), :, :, lanes],
+            ext.at[pl.ds(MARGIN + levels, MARGIN), :, :, lanes],
+            zs.at[n, 1],
+            zr.at[n, 1],
+            "lev",
+            jnp.maximum(lev - 1, 0),
+        )
+
+    def sum_copy(n, d):
+        return remote(
+            hsum.at[n], sums.at[n, d], ss.at[n, d], sr.at[n, d], "lev", jnp.maximum(lev - d, 0)
+        )
+
+    def heating(n, r):
+        lanes = pl.ds(n * span, span)
+        return [
+            ext[MARGIN + k, r, 0:1, lanes] * thickness[r, k : k + 1, lanes]
+            for k in range(levels)
+        ]
+
+    for n in range(chunks):
+        lanes = pl.ds(n * span, span)
+        for c in back[n]:
+            c.wait_recv()
+
+        @pl.when(lev < levs - 1)
+        def _():
+            up_copy(n).start()
+
+        @pl.when(lev > 0)
+        def _():
+            down_copy(n).start()
+
+        for r in range(rows):
+            heat = heating(n, r)
+            hsum[n, r : r + 1, :] = functools.reduce(add_terms, heat)
+        for d in range(1, levs):
+
+            @pl.when(lev >= d)
+            def _():
+                sum_copy(n, d).start()
+
+    for n in range(chunks):
+        lanes = pl.ds(n * span, span)
+
+        @pl.when(lev > 0)
+        def _():
+            up_copy(n).wait_recv()
+
+        @pl.when(lev < levs - 1)
+        def _():
+            down_copy(n).wait_recv()
+
+        @pl.when(lev == 0)
+        def _():
+            for m in range(MARGIN):
+                ext[m, :, :, lanes] = ext[MARGIN, :, :, lanes]
+
+        @pl.when(lev == levs - 1)
+        def _():
+            for m in range(MARGIN):
+                ext[MARGIN + levels + m, :, :, lanes] = ext[MARGIN + levels - 1, :, :, lanes]
+
+        for r in range(rows):
+            q = [ext[m, r, :, lanes] for m in range(levels + 2 * MARGIN)]
+            edge = {
+                m: (7.0 * (q[m - 1] + q[m]) - (q[m - 2] + q[m + 1])) * (1.0 / 12.0)
+                for m in range(2, levels + 2 * MARGIN - 1)
+            }
+            results = []
+            for k in range(levels):
+                delta = jnp.broadcast_to(rall[0, r, k : k + 1, lanes], q[0].shape)
+                weight = jnp.broadcast_to(rall[1, r, k : k + 1, lanes], q[0].shape)
+                s = k + MARGIN
+                centre, left, right = q[s - 2], edge[s - 2], edge[s - 1]
+                for o in range(-1, 3):
+                    chosen = delta == float(o)
+                    centre = jnp.where(chosen, q[s + o], centre)
+                    left = jnp.where(chosen, edge[s + o], left)
+                    right = jnp.where(chosen, edge[s + o + 1], right)
+                curve = 6.0 * centre - 3.0 * (left + right)
+                value = left + weight * ((right - left) + curve * (1.0 - weight))
+                for f in range(count):
+                    out[f, r, k : k + 1, lanes] = value[f : f + 1]
+
+        deep[...] = jnp.zeros_like(deep)
+        for d in range(1, levs):
+
+            @pl.when(lev + d < levs)
+            def _():
+                sum_copy(n, d).wait_recv()
+                deep[...] += sums[n, d]
+
+        for r in range(rows):
+            heat = heating(n, r)
+            below = surface[r : r + 1, lanes] + deep[r : r + 1, :]
+            for k in range(levels - 1, -1, -1):
+                geo[r, k : k + 1, lanes] = below + 0.5 * heat[k]
+                below = below + heat[k]
+
+    for c in fwd + first:
+        c.wait_send()
+    for n in range(chunks):
+        for c in back[n]:
+            c.wait_send()
+
+        @pl.when(lev < levs - 1)
+        def _():
+            up_copy(n).wait_send()
+
+        @pl.when(lev > 0)
+        def _():
+            down_copy(n).wait_send()
+
+        for d in range(1, levs):
+
+            @pl.when(lev >= d)
+            def _():
+                sum_copy(n, d).wait_send()
+
+
+def fused(lats, levs, chunks, state, courant, offsets, thickness, surface, level, weight):
+    count, rows, levels, width = state.shape
+    piece = level.shape[2]
+    slab = rows * lats
+    span = width // chunks
+    f32 = jnp.float32
+    dma = pltpu.SemaphoreType.DMA
+    vmem = pl.BlockSpec(memory_space=pltpu.VMEM)
+    return pl.pallas_call(
+        functools.partial(kernel, lats, levs, chunks),
+        out_shape=(
+            jax.ShapeDtypeStruct(state.shape, f32),
+            jax.ShapeDtypeStruct(thickness.shape, f32),
+        ),
+        in_specs=[vmem] * 7,
+        out_specs=(vmem, vmem),
+        scratch_shapes=[
+            pltpu.VMEM((levels, rows, count + 2, width), f32),
+            pltpu.VMEM((levels, rows, 2, width), jnp.int32),
+            pltpu.VMEM((slab + 4, count + 2, width), f32),
+            pltpu.VMEM((slab + 2, 2, width), jnp.int32),
+            pltpu.VMEM((slab + 4, count + 2, width), f32),
+            pltpu.VMEM((slab, count, width), f32),
+            pltpu.VMEM((levels + 2 * MARGIN, rows, count, width), f32),
+            pltpu.VMEM((levs, 2, rows, levels, piece), f32),
+            pltpu.VMEM((levs, 2, rows, levels, piece), f32),
+            pltpu.VMEM((2, rows, levels, width), f32),
+            pltpu.VMEM((chunks, rows, span), f32),
+            pltpu.VMEM((chunks, levs, rows, span), f32),
+            pltpu.VMEM((rows, span), f32),
+            dma((lats,)),
+            dma((lats,)),
+            dma((lats,)),
+            dma((lats,)),
+            dma((chunks, lats)),
+            dma((chunks, lats)),
+            dma((chunks, 2)),
+            dma((chunks, 2)),
+            dma((levs,)),
+            dma((levs,)),
+            dma((chunks, levs)),
+            dma((chunks, levs)),
+        ],
+        compiler_params=pltpu.CompilerParams(collective_id=0, has_side_effects=True),
+    )(state, courant, offsets, thickness, surface, level, weight)
+
+
 def solution(mesh):
     in_specs = (
         P(None, "lat", "lev", None),
@@ -122,6 +490,15 @@
         P("lat", None, "lev"),
     )
     out_specs = (P(None, "lat", "lev", None), P("lat", "lev", None))
+    lats, levs = mesh.shape["lat"], mesh.shape["lev"]
+
+    def body(state, *rest):
+        levels, width = state.shape[2:]
+        chunks = next((c for c in (3, 2, 1) if width % (c * 128) == 0), 0)
+        if levels != lats or levels < MARGIN or chunks == 0 or levs < 2:
+            return per_device(state, *rest)
+        return fused(lats, levs, chunks, state, *rest)
+
     return jax.shard_map(
-        per_device, mesh=mesh, in_specs=in_specs, out_specs=out_specs, check_vma=False
+        body, mesh=mesh, in_specs=in_specs, out_specs=out_specs, check_vma=False
     )

time: 88.6 us -> 37.7 us (0.43)
  the two profiles are of different devices: /device:TPU:5 before, /device:TPU:0 now
where the time goes in v1:
time: 37.7 us; the launch traced here: 37.6 us
  Pallas kernels  34.5 us (92%)
  local copies, waits for them, and re-layouts  2.37 us (6%)
  between operations  0.65 us (2%)
    pallas_call x1, Pallas kernels, fused(): pl.pallas_call(functools.partial(kernel, lats, levs, chunks), out_shape=(...  34.5 us
    unnamed x4, local copies, waits for them, and re-layouts  2.37 us

profile of v1, /device:TPU:0, one launch (start us, length us, event | category | flops | bytes accessed | tf_op | source)
XLA Modules:
  0.0 37.6 jit_solution(10494836314500970448)
XLA Ops:
  0.6 34.5 %shard_map.86 = (f32[6,3,4,1152]{3,2,1,0:T(4,128)}, f32[3,4,1152]{2,1,0:T(4,128)}) custom-call(f32[6,3,4,1152]{3,2,1,0:T(4,128)} %state.1, f32[2,3,4,1152]{3,2,1,0:T(4,128)} %courant.1, s32[2,3,4,1152]{3,2,1,0:T(4,128)} %offsets.1, f32[3,4,1152]{2,1,0:T(4,128)} %thickness.1, f32[3,1152]{1,0:T(4,128)} %surface.1, s32[3,32,144]{2,1,0:T(8,128)} %remap_level.1, ...), custom_call_target="tpu_custom_call" | custom-call | tf_op jit(solution)/shard_map/pallas_call | solution.py:443
  35.2 0.0 copy-start
  35.2 1.7 %copy.11 = f32[6,3,4,1152]{3,2,1,0:T(4,128)} copy(f32[6,3,4,1152]{3,2,1,0:T(4,128)} %get-tuple-element.4) | data formatting | bytes 663552
  36.9 0.0 copy-done
  36.9 0.6 %copy.12 = f32[3,4,1152]{2,1,0:T(4,128)} copy(f32[3,4,1152]{2,1,0:T(4,128)S(1)} %copy-done) | data formatting | bytes 110592
Async XLA Ops:
  35.2 1.8 %copy-start = (f32[3,4,1152]{2,1,0:T(4,128)S(1)}, f32[3,4,1152]{2,1,0:T(4,128)}, u32[]{:S(2)}) copy-start(f32[3,4,1152]{2,1,0:T(4,128)} %get-tuple-element.5) | copy-start | bytes 165892

commit v2 on v1

--- a/solution.py
+++ b/solution.py
@@ -116,6 +116,7 @@
 
 
 MARGIN = 4
+UNROLL = 3
 MESH = pl.DeviceIdType.MESH
 
 
@@ -130,64 +131,104 @@
     )
 
 
-def kernel(
-    lats,
-    levs,
-    chunks,
-    state,
-    courant,
-    offsets,
-    thickness,
-    surface,
-    remap_level,
-    remap_weight,
-    out,
-    geo,
-    pack,
-    pack_off,
-    work,
-    work_off,
-    mid,
-    ret,
-    ext,
-    rpack,
-    rrecv,
-    rall,
-    hsum,
-    sums,
-    deep,
-    fs,
-    fr,
-    gs,
-    gr,
-    bs,
-    br,
-    zs,
-    zr,
-    rs,
-    rr,
-    ss,
-    sr,
-):
+def compact(count):
+    sizes, size = [8] * (count // 8), 4
+    count %= 8
+    while count:
+        if count >= size:
+            sizes.append(size)
+            count -= size
+        size //= 2
+    return sizes
+
+
+def kernel(lats, levs, chunks, *refs):
+    (
+        h_state,
+        h_courant,
+        h_offsets,
+        h_thickness,
+        h_surface,
+        h_level,
+        h_weight,
+        out,
+        geo,
+        state,
+        courant,
+        offsets,
+        thickness,
+        surface,
+        remap_level,
+        remap_weight,
+        pack,
+        pack_off,
+        work,
+        work_off,
+        mid,
+        rpack,
+        rrecv,
+        rall,
+        hsum,
+        psum,
+        csum,
+        sums,
+        deep,
+        ins,
+        fs,
+        fr,
+        gs,
+        gr,
+        bs,
+        br,
+        zs,
+        zr,
+        rs,
+        rr,
+        ps,
+        pr,
+        ss,
+        sr,
+    ) = refs[:44]
     count, rows, levels, width = state.shape
+    groups = compact(count)
+    parts = len(groups)
+    rets, exts = refs[44 : 44 + parts], refs[44 + parts :]
     slab = rows * lats
     piece = remap_level.shape[2]
     span = width // chunks
     me = lax.axis_index("lat")
     lev = lax.axis_index("lev")
-
+    core = lax.rem(lev, 2)
+
+    loads = [
+        pltpu.make_async_copy(a, b, ins.at[n])
+        for n, (a, b) in enumerate(
+            (
+                (h_state, state),
+                (h_courant, courant),
+                (h_offsets, offsets),
+                (h_level, remap_level),
+                (h_weight, remap_weight),
+                (h_thickness, thickness),
+                (h_surface, surface),
+            )
+        )
+    ]
+    for c in loads:
+        c.start()
     barrier = pltpu.get_barrier_semaphore()
+    for d in range(1, levs):
+        pl.semaphore_signal(
+            barrier, inc=1, device_id={"lev": lax.rem(lev + d, levs)}, device_id_type=MESH
+        )
     for d in range(1, lats):
         pl.semaphore_signal(
             barrier, inc=1, device_id={"lat": lax.rem(me + d, lats)}, device_id_type=MESH
         )
-    for d in range(1, levs):
-        pl.semaphore_signal(
-            barrier, inc=1, device_id={"lev": lax.rem(lev + d, levs)}, device_id_type=MESH
-        )
-
-    def pack_level(level):
-        at = pl.ds(level, 1)
+    for c in loads[:3]:
+        c.wait()
+    for level in range(levels):
+        at = slice(level, level + 1)
         for r in range(rows):
             for f in range(count):
                 pack[level, r, f : f + 1, :] = state[f, r, at, :]
@@ -195,12 +236,10 @@
                 pack[level, r, count + f : count + f + 1, :] = courant[f, r, at, :]
                 pack_off[level, r, f : f + 1, :] = offsets[f, r, at, :]
 
+    pl.semaphore_wait(barrier, lats + levs - 2)
     fwd = []
     for d in range(1, lats):
         peer = lax.rem(me + d, lats)
-        pack_level(peer)
-        if d == 1:
-            pl.semaphore_wait(barrier, lats + levs - 2)
         a = remote(
             pack.at[peer], work.at[pl.ds(2 + rows * me, rows)], fs.at[d], fr.at[d], "lat", peer
         )
@@ -211,6 +250,8 @@
         b.start()
         fwd += [a, b]
 
+    for c in loads[3:]:
+        c.wait()
     first = []
     for p in range(levs):
         for r in range(rows):
@@ -225,7 +266,6 @@
         first.append(c)
     rrecv[lev] = rpack[lev]
 
-    pack_level(me)
     for r in range(rows):
         work[2 + rows * me + r] = pack[me, r]
         work_off[1 + rows * me + r] = pack_off[me, r]
@@ -262,13 +302,16 @@
             store(j, q - (north - south) - (east - west))
             return north
 
-        lax.fori_loop(0, slab, face, jnp.zeros(whole, jnp.float32))
+        lax.fori_loop(0, slab, face, jnp.zeros(whole, jnp.float32), unroll=UNROLL)
 
     def store_mid(j, value):
         mid[j + 2] = value
 
     def store_ret(j, value):
-        ret[j] = value[:count]
+        lo = 0
+        for ref, size in zip(rets, groups):
+            ref[j] = value[lo : lo + size]
+            lo += size
 
     substep(work, store_mid)
     substep(mid, store_ret)
@@ -279,134 +322,150 @@
         some = []
         for d in range(1, lats):
             peer = lax.rem(me + d, lats)
-            c = remote(
-                ret.at[pl.ds(rows * peer, rows), :, lanes],
-                ext.at[MARGIN + me, :, :, lanes],
-                bs.at[n, d],
-                br.at[n, d],
-                "lat",
-                peer,
-            )
-            c.start()
-            some.append(c)
+            for g in range(parts):
+                c = remote(
+                    rets[g].at[pl.ds(rows * peer, rows), :, lanes],
+                    exts[g].at[MARGIN + me, :, :, lanes],
+                    bs.at[n, d, g],
+                    br.at[n, d, g],
+                    "lat",
+                    peer,
+                )
+                c.start()
+                some.append(c)
         back.append(some)
     for r in range(rows):
-        ext[MARGIN + me, r] = ret[rows * me + r]
+        for ret, ext in zip(rets, exts):
+            ext[MARGIN + me, r] = ret[rows * me + r]
     for c in first:
         c.wait_recv()
     for p in range(levs):
         rall[:, :, :, p * piece : (p + 1) * piece] = rrecv[p]
 
-    def up_copy(n):
+    def level_copies(n, way):
         lanes = pl.ds(n * span, span)
-        return remote(
-            ext.at[pl.ds(levels, MARGIN), :, :, lanes],
-            ext.at[pl.ds(0, MARGIN), :, :, lanes],
-            zs.at[n, 0],
-            zr.at[n, 0],
-            "lev",
-            jnp.minimum(lev + 1, levs - 1),
-        )
-
-    def down_copy(n):
-        lanes = pl.ds(n * span, span)
-        return remote(
-            ext.at[pl.ds(MARGIN, MARGIN), :, :, lanes],
-            ext.at[pl.ds(MARGIN + levels, MARGIN), :, :, lanes],
-            zs.at[n, 1],
-            zr.at[n, 1],
-            "lev",
-            jnp.maximum(lev - 1, 0),
-        )
+        source, target = ((levels, 0), (MARGIN, MARGIN + levels))[way]
+        peer = (jnp.minimum(lev + 1, levs - 1), jnp.maximum(lev - 1, 0))[way]
+        return [
+            remote(
+                exts[g].at[pl.ds(source, MARGIN), :, :, lanes],
+                exts[g].at[pl.ds(target, MARGIN), :, :, lanes],
+                zs.at[n, way, g],
+                zr.at[n, way, g],
+                "lev",
+                peer,
+            )
+            for g in range(parts)
+        ]
+
+    def pair_copy(n):
+        return remote(hsum.at[n], psum.at[n], ps.at[n], pr.at[n], "lev", lev + 1 - 2 * core)
 
     def sum_copy(n, d):
         return remote(
-            hsum.at[n], sums.at[n, d], ss.at[n, d], sr.at[n, d], "lev", jnp.maximum(lev - d, 0)
+            csum.at[n], sums.at[n, d], ss.at[n, d], sr.at[n, d], "lev", jnp.maximum(lev - 2 * d, core)
         )
 
     def heating(n, r):
         lanes = pl.ds(n * span, span)
         return [
-            ext[MARGIN + k, r, 0:1, lanes] * thickness[r, k : k + 1, lanes]
+            exts[0][MARGIN + k, r, 0:1, lanes] * thickness[r, k : k + 1, lanes]
             for k in range(levels)
         ]
+
+    def pass_on(n):
+        pair_copy(n).wait_recv()
+        csum[n] = hsum[n] + psum[n]
+        for d in range(1, levs // 2):
+
+            @pl.when(lev >= 2 * d)
+            def _():
+                sum_copy(n, d).start()
 
     for n in range(chunks):
         lanes = pl.ds(n * span, span)
         for c in back[n]:
             c.wait_recv()
+        for r in range(rows):
+            hsum[n, r] = functools.reduce(add_terms, heating(n, r))
+        pair_copy(n).start()
 
         @pl.when(lev < levs - 1)
         def _():
-            up_copy(n).start()
+            for c in level_copies(n, 0):
+                c.start()
 
         @pl.when(lev > 0)
         def _():
-            down_copy(n).start()
-
-        for r in range(rows):
-            heat = heating(n, r)
-            hsum[n, r : r + 1, :] = functools.reduce(add_terms, heat)
-        for d in range(1, levs):
-
-            @pl.when(lev >= d)
-            def _():
-                sum_copy(n, d).start()
+            for c in level_copies(n, 1):
+                c.start()
+
+        if n > 0:
+            pass_on(n - 1)
+    pass_on(chunks - 1)
 
     for n in range(chunks):
         lanes = pl.ds(n * span, span)
 
         @pl.when(lev > 0)
         def _():
-            up_copy(n).wait_recv()
+            for c in level_copies(n, 0):
+                c.wait_recv()
 
         @pl.when(lev < levs - 1)
         def _():
-            down_copy(n).wait_recv()
+            for c in level_copies(n, 1):
+                c.wait_recv()
 
         @pl.when(lev == 0)
         def _():
-            for m in range(MARGIN):
-                ext[m, :, :, lanes] = ext[MARGIN, :, :, lanes]
+            for ext in exts:
+                for m in range(MARGIN):
+                    ext[m, :, :, lanes] = ext[MARGIN, :, :, lanes]
 
         @pl.when(lev == levs - 1)
         def _():
-            for m in range(MARGIN):
-                ext[MARGIN + levels + m, :, :, lanes] = ext[MARGIN + levels - 1, :, :, lanes]
+            for ext in exts:
+                for m in range(MARGIN):
+                    ext[MARGIN + levels + m, :, :, lanes] = ext[MARGIN + levels - 1, :, :, lanes]
 
         for r in range(rows):
-            q = [ext[m, r, :, lanes] for m in range(levels + 2 * MARGIN)]
-            edge = {
-                m: (7.0 * (q[m - 1] + q[m]) - (q[m - 2] + q[m + 1])) * (1.0 / 12.0)
-                for m in range(2, levels + 2 * MARGIN - 1)
-            }
-            results = []
-            for k in range(levels):
-                delta = jnp.broadcast_to(rall[0, r, k : k + 1, lanes], q[0].shape)
-                weight = jnp.broadcast_to(rall[1, r, k : k + 1, lanes], q[0].shape)
-                s = k + MARGIN
-                centre, left, right = q[s - 2], edge[s - 2], edge[s - 1]
-                for o in range(-1, 3):
-                    chosen = delta == float(o)
-                    centre = jnp.where(chosen, q[s + o], centre)
-                    left = jnp.where(chosen, edge[s + o], left)
-                    right = jnp.where(chosen, edge[s + o + 1], right)
-                curve = 6.0 * centre - 3.0 * (left + right)
-                value = left + weight * ((right - left) + curve * (1.0 - weight))
-                for f in range(count):
-                    out[f, r, k : k + 1, lanes] = value[f : f + 1]
-
-        deep[...] = jnp.zeros_like(deep)
-        for d in range(1, levs):
-
-            @pl.when(lev + d < levs)
+            lo = 0
+            for ext, size in zip(exts, groups):
+                q = [ext[m, r, :, lanes] for m in range(levels + 2 * MARGIN)]
+                edge = {
+                    m: (7.0 * (q[m - 1] + q[m]) - (q[m - 2] + q[m + 1])) * (1.0 / 12.0)
+                    for m in range(2, levels + 2 * MARGIN - 1)
+                }
+                for k in range(levels):
+                    delta = jnp.broadcast_to(rall[0, r, k : k + 1, lanes], q[0].shape)
+                    weight = jnp.broadcast_to(rall[1, r, k : k + 1, lanes], q[0].shape)
+                    s = k + MARGIN
+                    centre, left, right = q[s - 2], edge[s - 2], edge[s - 1]
+                    for o in range(-1, 3):
+                        chosen = delta == float(o)
+                        centre = jnp.where(chosen, q[s + o], centre)
+                        left = jnp.where(chosen, edge[s + o], left)
+                        right = jnp.where(chosen, edge[s + o + 1], right)
+                    curve = 6.0 * centre - 3.0 * (left + right)
+                    value = left + weight * ((right - left) + curve * (1.0 - weight))
+                    for f in range(size):
+                        out[lo + f, r, k : k + 1, lanes] = value[f : f + 1]
+                lo += size
+
+    for n in range(chunks):
+        lanes = pl.ds(n * span, span)
+        deep[...] = jnp.where(core == 0, psum[n], jnp.zeros_like(deep))
+        for d in range(1, levs // 2):
+
+            @pl.when(lev + 2 * d < levs)
             def _():
                 sum_copy(n, d).wait_recv()
                 deep[...] += sums[n, d]
 
         for r in range(rows):
             heat = heating(n, r)
-            below = surface[r : r + 1, lanes] + deep[r : r + 1, :]
+            below = surface[r : r + 1, lanes] + deep[r]
             for k in range(levels - 1, -1, -1):
                 geo[r, k : k + 1, lanes] = below + 0.5 * heat[k]
                 below = below + heat[k]
@@ -416,67 +475,74 @@
     for n in range(chunks):
         for c in back[n]:
             c.wait_send()
+        pair_copy(n).wait_send()
 
         @pl.when(lev < levs - 1)
         def _():
-            up_copy(n).wait_send()
+            for c in level_copies(n, 0):
+                c.wait_send()
 
         @pl.when(lev > 0)
         def _():
-            down_copy(n).wait_send()
-
-        for d in range(1, levs):
-
-            @pl.when(lev >= d)
+            for c in level_copies(n, 1):
+                c.wait_send()
+
+        for d in range(1, levs // 2):
+
+            @pl.when(lev >= 2 * d)
             def _():
                 sum_copy(n, d).wait_send()
 
 
-def fused(lats, levs, chunks, state, courant, offsets, thickness, surface, level, weight):
+def fused(lats, levs, chunks, *args):
+    state, courant, offsets, thickness, surface, level, weight = args
     count, rows, levels, width = state.shape
     piece = level.shape[2]
     slab = rows * lats
     span = width // chunks
     f32 = jnp.float32
     dma = pltpu.SemaphoreType.DMA
-    vmem = pl.BlockSpec(memory_space=pltpu.VMEM)
+    groups = compact(count)
+    parts = len(groups)
     return pl.pallas_call(
         functools.partial(kernel, lats, levs, chunks),
-        out_shape=(
-            jax.ShapeDtypeStruct(state.shape, f32),
-            jax.ShapeDtypeStruct(thickness.shape, f32),
-        ),
-        in_specs=[vmem] * 7,
-        out_specs=(vmem, vmem),
+        out_shape=(pltpu.VMEM(state.shape, f32), pltpu.VMEM(thickness.shape, f32)),
+        in_specs=[pl.BlockSpec(memory_space=pl.ANY)] * 7,
         scratch_shapes=[
+            *(pltpu.VMEM(x.shape, x.dtype) for x in args),
             pltpu.VMEM((levels, rows, count + 2, width), f32),
             pltpu.VMEM((levels, rows, 2, width), jnp.int32),
             pltpu.VMEM((slab + 4, count + 2, width), f32),
             pltpu.VMEM((slab + 2, 2, width), jnp.int32),
             pltpu.VMEM((slab + 4, count + 2, width), f32),
-            pltpu.VMEM((slab, count, width), f32),
-            pltpu.VMEM((levels + 2 * MARGIN, rows, count, width), f32),
             pltpu.VMEM((levs, 2, rows, levels, piece), f32),
             pltpu.VMEM((levs, 2, rows, levels, piece), f32),
             pltpu.VMEM((2, rows, levels, width), f32),
-            pltpu.VMEM((chunks, rows, span), f32),
-            pltpu.VMEM((chunks, levs, rows, span), f32),
-            pltpu.VMEM((rows, span), f32),
+            pltpu.VMEM((chunks, rows, 1, span), f32),
+            pltpu.VMEM((chunks, rows, 1, span), f32),
+            pltpu.VMEM((chunks, rows, 1, span), f32),
+            pltpu.VMEM((chunks, levs // 2, rows, 1, span), f32),
+            pltpu.VMEM((rows, 1, span), f32),
+            dma((7,)),
             dma((lats,)),
             dma((lats,)),
             dma((lats,)),
             dma((lats,)),
-            dma((chunks, lats)),
-            dma((chunks, lats)),
-            dma((chunks, 2)),
-            dma((chunks, 2)),
+            dma((chunks, lats, parts)),
+            dma((chunks, lats, parts)),
+            dma((chunks, 2, parts)),
+            dma((chunks, 2, parts)),
             dma((levs,)),
             dma((levs,)),
-            dma((chunks, levs)),
-            dma((chunks, levs)),
+            dma((chunks,)),
+            dma((chunks,)),
+            dma((chunks, levs // 2)),
+            dma((chunks, levs // 2)),
+            *(pltpu.VMEM((slab, g, width), f32) for g in groups),
+            *(pltpu.VMEM((levels + 2 * MARGIN, rows, g, width), f32) for g in groups),
         ],
         compiler_params=pltpu.CompilerParams(collective_id=0, has_side_effects=True),
-    )(state, courant, offsets, thickness, surface, level, weight)
+    )(*args)
 
 
 def solution(mesh):
@@ -495,7 +561,7 @@
     def body(state, *rest):
         levels, width = state.shape[2:]
         chunks = next((c for c in (3, 2, 1) if width % (c * 128) == 0), 0)
-        if levels != lats or levels < MARGIN or chunks == 0 or levs < 2:
+        if levels != lats or levels < MARGIN or chunks == 0 or levs % 2:
             return per_device(state, *rest)
         return fused(lats, levs, chunks, state, *rest)
 

time: 37.7 us -> 30.5 us (0.81)
  Pallas kernels: 34.5 us -> 28.3 us
  local copies, waits for them, and re-layouts: 2.37 us -> 1.35 us
    pallas_call x1, Pallas kernels: 34.5 us -> 28.3 us  [fused(): pl.pallas_call(functools.partial(kernel, lats, levs, chunks), out_shape=(...]
    unnamed x4 -> x2, local copies, waits for them, and re-layouts: 2.37 us -> 1.35 us
where the time goes in v2:
time: 30.5 us; the launch traced here: 30.3 us
  Pallas kernels  28.3 us (93%)
  local copies, waits for them, and re-layouts  1.35 us (4%)
  between operations  0.64 us (2%)
    pallas_call x1, Pallas kernels, fused(): pl.pallas_call(functools.partial(kernel, lats, levs, chunks), out_shape=(...  28.3 us
    unnamed x2, local copies, waits for them, and re-layouts  1.35 us

profile of v2, /device:TPU:0, one launch (start us, length us, event | category | flops | bytes accessed | tf_op | source)
XLA Modules:
  0.0 30.3 jit_solution(14868024992963429912)
XLA Ops:
  0.6 28.3 %shard_map.86 = (f32[6,3,4,1152]{3,2,1,0:T(4,128)S(1)}, f32[3,4,1152]{2,1,0:T(4,128)S(1)}) custom-call(f32[6,3,4,1152]{3,2,1,0:T(4,128)} %refs_0_.1, f32[2,3,4,1152]{3,2,1,0:T(4,128)} %refs_1_.1, s32[2,3,4,1152]{3,2,1,0:T(4,128)} %refs_2_.1, f32[3,4,1152]{2,1,0:T(4,128)} %refs_3_.1, f32[3,1152]{1,0:T(4,128)} %refs_4_.1, s32[3,32,144]{2,1,0:T(8,128)} %refs_5_.1, ...), custom_call_target="tpu_custom_call" | custom-call | tf_op jit(solution)/shard_map/pallas_call | solution.py:507
  29.0 0.7 %copy.11 = f32[6,3,4,1152]{3,2,1,0:T(4,128)} copy(f32[6,3,4,1152]{3,2,1,0:T(4,128)S(1)} %get-tuple-element.2) | data formatting | bytes 663552
  29.7 0.6 %copy.12 = f32[3,4,1152]{2,1,0:T(4,128)} copy(f32[3,4,1152]{2,1,0:T(4,128)S(1)} %get-tuple-element.3) | data formatting | bytes 110592

commit v3 on v2

--- a/solution.py
+++ b/solution.py
@@ -160,11 +160,8 @@
         surface,
         remap_level,
         remap_weight,
-        pack,
-        pack_off,
-        work,
-        work_off,
-        mid,
+        pack_c,
+        work_c,
         rpack,
         rrecv,
         rall,
@@ -176,8 +173,6 @@
         ins,
         fs,
         fr,
-        gs,
-        gr,
         bs,
         br,
         zs,
@@ -188,11 +183,13 @@
         pr,
         ss,
         sr,
-    ) = refs[:44]
+    ) = refs[:39]
     count, rows, levels, width = state.shape
     groups = compact(count)
     parts = len(groups)
-    rets, exts = refs[44 : 44 + parts], refs[44 + parts :]
+    packs, works, mids, rets, exts = (
+        refs[39 + n * parts : 39 + (n + 1) * parts] for n in range(5)
+    )
     slab = rows * lats
     piece = remap_level.shape[2]
     span = width // chunks
@@ -230,25 +227,41 @@
     for level in range(levels):
         at = slice(level, level + 1)
         for r in range(rows):
-            for f in range(count):
-                pack[level, r, f : f + 1, :] = state[f, r, at, :]
-            for f in range(2):
-                pack[level, r, count + f : count + f + 1, :] = courant[f, r, at, :]
-                pack_off[level, r, f : f + 1, :] = offsets[f, r, at, :]
+            f = 0
+            for ref, size in zip(packs, groups):
+                for g in range(size):
+                    ref[level, r, g : g + 1, :] = state[f, r, at, :]
+                    f += 1
+            for g in range(2):
+                pack_c[level, r, g : g + 1, :] = courant[g, r, at, :]
+                pack_c[level, r, g + 2 : g + 3, :] = offsets[g, r, at, :].astype(jnp.float32)
 
     pl.semaphore_wait(barrier, lats + levs - 2)
-    fwd = []
-    for d in range(1, lats):
-        peer = lax.rem(me + d, lats)
-        a = remote(
-            pack.at[peer], work.at[pl.ds(2 + rows * me, rows)], fs.at[d], fr.at[d], "lat", peer
-        )
-        b = remote(
-            pack_off.at[peer], work_off.at[pl.ds(1 + rows * me, rows)], gs.at[d], gr.at[d], "lat", peer
-        )
-        a.start()
-        b.start()
-        fwd += [a, b]
+    fwd = [[] for _ in groups]
+    for g in range(parts):
+        for d in range(1, lats):
+            peer = lax.rem(me + d, lats)
+            if g == 0:
+                c = remote(
+                    pack_c.at[peer],
+                    work_c.at[pl.ds(1 + rows * me, rows)],
+                    fs.at[parts, d],
+                    fr.at[parts, d],
+                    "lat",
+                    peer,
+                )
+                c.start()
+                fwd[g].append(c)
+            c = remote(
+                packs[g].at[peer],
+                works[g].at[pl.ds(2 + rows * me, rows)],
+                fs.at[g, d],
+                fr.at[g, d],
+                "lat",
+                peer,
+            )
+            c.start()
+            fwd[g].append(c)
 
     for c in loads[3:]:
         c.wait()
@@ -267,62 +280,54 @@
     rrecv[lev] = rpack[lev]
 
     for r in range(rows):
-        work[2 + rows * me + r] = pack[me, r]
-        work_off[1 + rows * me + r] = pack_off[me, r]
-    blank = jnp.zeros(work.shape[1:], jnp.float32)
-    for r in (0, 1, slab + 2, slab + 3):
-        work[r] = blank
-        mid[r] = blank
-
-    for c in fwd:
-        c.wait_recv()
-
-    whole = work.shape[1:]
-
-    def substep(source, store):
+        work_c[1 + rows * me + r] = pack_c[me, r]
+        for work, ref in zip(works, packs):
+            work[2 + rows * me + r] = ref[me, r]
+    for work, mid in zip(works, mids):
+        blank = jnp.zeros(work.shape[1:], jnp.float32)
+        for r in (0, 1, slab + 2, slab + 3):
+            work[r] = blank
+            mid[r] = blank
+
+    def substep(source, target, shift):
+        whole = source.shape[1:]
+
         def face(j, south):
             q = source[j + 2]
-            o0 = jnp.broadcast_to(work_off[j + 1, 0:1, :], whole)
-            o1 = jnp.broadcast_to(work_off[j + 1, 1:2, :], whole)
-            c0 = jnp.broadcast_to(work[j + 2, count : count + 1, :], whole)
-            c1 = jnp.broadcast_to(work[j + 2, count + 1 : count + 2, :], whole)
+            o0 = jnp.broadcast_to(work_c[j + 1, 2:3, :], whole)
+            o1 = jnp.broadcast_to(work_c[j + 1, 3:4, :], whole)
+            c0 = jnp.broadcast_to(work_c[j + 1, 0:1, :], whole)
+            c1 = jnp.broadcast_to(work_c[j + 1, 1:2, :], whole)
             up = jnp.where(
-                o0 <= 0,
-                jnp.where(o0 == 0, q, source[j + 1]),
-                jnp.where(o0 == 1, source[j + 3], source[j + 4]),
+                o0 < 0.5,
+                jnp.where(o0 == 0.0, q, source[j + 1]),
+                jnp.where(o0 == 1.0, source[j + 3], source[j + 4]),
             )
             north = c0 * up
             side = jnp.where(
-                o1 <= 0,
-                jnp.where(o1 == 0, q, pltpu.roll(q, 1, 1)),
-                jnp.where(o1 == 1, pltpu.roll(q, width - 1, 1), pltpu.roll(q, width - 2, 1)),
+                o1 < 0.5,
+                jnp.where(o1 == 0.0, q, pltpu.roll(q, 1, 1)),
+                jnp.where(o1 == 1.0, pltpu.roll(q, width - 1, 1), pltpu.roll(q, width - 2, 1)),
             )
             east = c1 * side
             west = pltpu.roll(east, 1, 1)
-            store(j, q - (north - south) - (east - west))
+            target[j + shift] = q - (north - south) - (east - west)
             return north
 
         lax.fori_loop(0, slab, face, jnp.zeros(whole, jnp.float32), unroll=UNROLL)
 
-    def store_mid(j, value):
-        mid[j + 2] = value
-
-    def store_ret(j, value):
-        lo = 0
-        for ref, size in zip(rets, groups):
-            ref[j] = value[lo : lo + size]
-            lo += size
-
-    substep(work, store_mid)
-    substep(mid, store_ret)
-
     back = []
-    for n in range(chunks):
-        lanes = pl.ds(n * span, span)
-        some = []
-        for d in range(1, lats):
-            peer = lax.rem(me + d, lats)
-            for g in range(parts):
+    for g in range(parts):
+        for c in fwd[g]:
+            c.wait_recv()
+        substep(works[g], mids[g], 2)
+        substep(mids[g], rets[g], 0)
+        back.append([])
+        for n in range(chunks):
+            lanes = pl.ds(n * span, span)
+            some = []
+            for d in range(1, lats):
+                peer = lax.rem(me + d, lats)
                 c = remote(
                     rets[g].at[pl.ds(rows * peer, rows), :, lanes],
                     exts[g].at[MARGIN + me, :, :, lanes],
@@ -333,7 +338,7 @@
                 )
                 c.start()
                 some.append(c)
-        back.append(some)
+            back[g].append(some)
     for r in range(rows):
         for ret, ext in zip(rets, exts):
             ext[MARGIN + me, r] = ret[rows * me + r]
@@ -342,21 +347,18 @@
     for p in range(levs):
         rall[:, :, :, p * piece : (p + 1) * piece] = rrecv[p]
 
-    def level_copies(n, way):
+    def level_copy(n, way, g):
         lanes = pl.ds(n * span, span)
         source, target = ((levels, 0), (MARGIN, MARGIN + levels))[way]
         peer = (jnp.minimum(lev + 1, levs - 1), jnp.maximum(lev - 1, 0))[way]
-        return [
-            remote(
-                exts[g].at[pl.ds(source, MARGIN), :, :, lanes],
-                exts[g].at[pl.ds(target, MARGIN), :, :, lanes],
-                zs.at[n, way, g],
-                zr.at[n, way, g],
-                "lev",
-                peer,
-            )
-            for g in range(parts)
-        ]
+        return remote(
+            exts[g].at[pl.ds(source, MARGIN), :, :, lanes],
+            exts[g].at[pl.ds(target, MARGIN), :, :, lanes],
+            zs.at[n, way, g],
+            zr.at[n, way, g],
+            "lev",
+            peer,
+        )
 
     def pair_copy(n):
         return remote(hsum.at[n], psum.at[n], ps.at[n], pr.at[n], "lev", lev + 1 - 2 * core)
@@ -382,76 +384,73 @@
             def _():
                 sum_copy(n, d).start()
 
-    for n in range(chunks):
+    for g in range(parts):
+        for n in range(chunks):
+            for c in back[g][n]:
+                c.wait_recv()
+            if g == 0:
+                for r in range(rows):
+                    hsum[n, r] = functools.reduce(add_terms, heating(n, r))
+                pair_copy(n).start()
+
+            @pl.when(lev < levs - 1)
+            def _():
+                level_copy(n, 0, g).start()
+
+            @pl.when(lev > 0)
+            def _():
+                level_copy(n, 1, g).start()
+
+            if g == 0 and n > 0:
+                pass_on(n - 1)
+        if g == 0:
+            pass_on(chunks - 1)
+
+    def remap(g, n):
         lanes = pl.ds(n * span, span)
-        for c in back[n]:
-            c.wait_recv()
-        for r in range(rows):
-            hsum[n, r] = functools.reduce(add_terms, heating(n, r))
-        pair_copy(n).start()
+        ext, size, lo = exts[g], groups[g], sum(groups[:g])
+
+        @pl.when(lev > 0)
+        def _():
+            level_copy(n, 0, g).wait_recv()
 
         @pl.when(lev < levs - 1)
         def _():
-            for c in level_copies(n, 0):
-                c.start()
-
-        @pl.when(lev > 0)
-        def _():
-            for c in level_copies(n, 1):
-                c.start()
-
-        if n > 0:
-            pass_on(n - 1)
-    pass_on(chunks - 1)
-
-    for n in range(chunks):
-        lanes = pl.ds(n * span, span)
-
-        @pl.when(lev > 0)
-        def _():
-            for c in level_copies(n, 0):
-                c.wait_recv()
-
-        @pl.when(lev < levs - 1)
-        def _():
-            for c in level_copies(n, 1):
-                c.wait_recv()
+            level_copy(n, 1, g).wait_recv()
 
         @pl.when(lev == 0)
         def _():
-            for ext in exts:
-                for m in range(MARGIN):
-                    ext[m, :, :, lanes] = ext[MARGIN, :, :, lanes]
+            for m in range(MARGIN):
+                ext[m, :, :, lanes] = ext[MARGIN, :, :, lanes]
 
         @pl.when(lev == levs - 1)
         def _():
-            for ext in exts:
-                for m in range(MARGIN):
-                    ext[MARGIN + levels + m, :, :, lanes] = ext[MARGIN + levels - 1, :, :, lanes]
+            for m in range(MARGIN):
+                ext[MARGIN + levels + m, :, :, lanes] = ext[MARGIN + levels - 1, :, :, lanes]
 
         for r in range(rows):
-            lo = 0
-            for ext, size in zip(exts, groups):
-                q = [ext[m, r, :, lanes] for m in range(levels + 2 * MARGIN)]
-                edge = {
-                    m: (7.0 * (q[m - 1] + q[m]) - (q[m - 2] + q[m + 1])) * (1.0 / 12.0)
-                    for m in range(2, levels + 2 * MARGIN - 1)
-                }
-                for k in range(levels):
-                    delta = jnp.broadcast_to(rall[0, r, k : k + 1, lanes], q[0].shape)
-                    weight = jnp.broadcast_to(rall[1, r, k : k + 1, lanes], q[0].shape)
-                    s = k + MARGIN
-                    centre, left, right = q[s - 2], edge[s - 2], edge[s - 1]
-                    for o in range(-1, 3):
-                        chosen = delta == float(o)
-                        centre = jnp.where(chosen, q[s + o], centre)
-                        left = jnp.where(chosen, edge[s + o], left)
-                        right = jnp.where(chosen, edge[s + o + 1], right)
-                    curve = 6.0 * centre - 3.0 * (left + right)
-                    value = left + weight * ((right - left) + curve * (1.0 - weight))
-                    for f in range(size):
-                        out[lo + f, r, k : k + 1, lanes] = value[f : f + 1]
-                lo += size
+            q = [ext[m, r, :, lanes] for m in range(levels + 2 * MARGIN)]
+            edge = {
+                m: (7.0 * (q[m - 1] + q[m]) - (q[m - 2] + q[m + 1])) * (1.0 / 12.0)
+                for m in range(2, levels + 2 * MARGIN - 1)
+            }
+            for k in range(levels):
+                delta = jnp.broadcast_to(rall[0, r, k : k + 1, lanes], q[0].shape)
+                weight = jnp.broadcast_to(rall[1, r, k : k + 1, lanes], q[0].shape)
+                s = k + MARGIN
+                centre, left, right = q[s - 2], edge[s - 2], edge[s - 1]
+                for o in range(-1, 3):
+                    chosen = delta == float(o)
+                    centre = jnp.where(chosen, q[s + o], centre)
+                    left = jnp.where(chosen, edge[s + o], left)
+                    right = jnp.where(chosen, edge[s + o + 1], right)
+                curve = 6.0 * centre - 3.0 * (left + right)
+                value = left + weight * ((right - left) + curve * (1.0 - weight))
+                for f in range(size):
+                    out[lo + f, r, k : k + 1, lanes] = value[f : f + 1]
+
+    for n in range(chunks):
+        remap(0, n)
 
     for n in range(chunks):
         lanes = pl.ds(n * span, span)
@@ -470,22 +469,27 @@
                 geo[r, k : k + 1, lanes] = below + 0.5 * heat[k]
                 below = below + heat[k]
 
-    for c in fwd + first:
+    for g in range(1, parts):
+        for n in range(chunks):
+            remap(g, n)
+
+    for c in sum(fwd, first):
         c.wait_send()
     for n in range(chunks):
-        for c in back[n]:
-            c.wait_send()
+        for g in range(parts):
+            for c in back[g][n]:
+                c.wait_send()
         pair_copy(n).wait_send()
 
         @pl.when(lev < levs - 1)
         def _():
-            for c in level_copies(n, 0):
-                c.wait_send()
+            for g in range(parts):
+                level_copy(n, 0, g).wait_send()
 
         @pl.when(lev > 0)
         def _():
-            for c in level_copies(n, 1):
-                c.wait_send()
+            for g in range(parts):
+                level_copy(n, 1, g).wait_send()
 
         for d in range(1, levs // 2):
 
@@ -510,11 +514,8 @@
         in_specs=[pl.BlockSpec(memory_space=pl.ANY)] * 7,
         scratch_shapes=[
             *(pltpu.VMEM(x.shape, x.dtype) for x in args),
-            pltpu.VMEM((levels, rows, count + 2, width), f32),
-            pltpu.VMEM((levels, rows, 2, width), jnp.int32),
-            pltpu.VMEM((slab + 4, count + 2, width), f32),
-            pltpu.VMEM((slab + 2, 2, width), jnp.int32),
-            pltpu.VMEM((slab + 4, count + 2, width), f32),
+            pltpu.VMEM((levels, rows, 4, width), f32),
+            pltpu.VMEM((slab + 2, 4, width), f32),
             pltpu.VMEM((levs, 2, rows, levels, piece), f32),
             pltpu.VMEM((levs, 2, rows, levels, piece), f32),
             pltpu.VMEM((2, rows, levels, width), f32),
@@ -524,10 +525,8 @@
             pltpu.VMEM((chunks, levs // 2, rows, 1, span), f32),
             pltpu.VMEM((rows, 1, span), f32),
             dma((7,)),
-            dma((lats,)),
-            dma((lats,)),
-            dma((lats,)),
-            dma((lats,)),
+            dma((parts + 1, lats)),
+            dma((parts + 1, lats)),
             dma((chunks, lats, parts)),
             dma((chunks, lats, parts)),
             dma((chunks, 2, parts)),
@@ -538,6 +537,9 @@
             dma((chunks,)),
             dma((chunks, levs // 2)),
             dma((chunks, levs // 2)),
+            *(pltpu.VMEM((levels, rows, g, width), f32) for g in groups),
+            *(pltpu.VMEM((slab + 4, g, width), f32) for g in groups),
+            *(pltpu.VMEM((slab + 4, g, width), f32) for g in groups),
             *(pltpu.VMEM((slab, g, width), f32) for g in groups),
             *(pltpu.VMEM((levels + 2 * MARGIN, rows, g, width), f32) for g in groups),
         ],

time: 30.5 us -> 29.4 us (0.964)
  Pallas kernels: 28.3 us -> 27.3 us
    pallas_call x1, Pallas kernels: 28.3 us -> 27.3 us  [fused(): pl.pallas_call(functools.partial(kernel, lats, levs, chunks), out_shape=(...]
where the time goes in v3:
time: 29.4 us; the launch traced here: 29.2 us
  Pallas kernels  27.3 us (93%)
  local copies, waits for them, and re-layouts  1.35 us (5%)
  between operations  0.64 us (2%)
    pallas_call x1, Pallas kernels, fused(): pl.pallas_call(functools.partial(kernel, lats, levs, chunks), out_shape=(...  27.3 us
    unnamed x2, local copies, waits for them, and re-layouts  1.35 us

profile of v3, /device:TPU:0, one launch (start us, length us, event | category | flops | bytes accessed | tf_op | source)
XLA Modules:
  0.0 29.2 jit_solution(2219107105318578950)
XLA Ops:
  0.6 27.3 %shard_map.86 = (f32[6,3,4,1152]{3,2,1,0:T(4,128)S(1)}, f32[3,4,1152]{2,1,0:T(4,128)S(1)}) custom-call(f32[6,3,4,1152]{3,2,1,0:T(4,128)} %refs_0_.1, f32[2,3,4,1152]{3,2,1,0:T(4,128)} %refs_1_.1, s32[2,3,4,1152]{3,2,1,0:T(4,128)} %refs_2_.1, f32[3,4,1152]{2,1,0:T(4,128)} %refs_3_.1, f32[3,1152]{1,0:T(4,128)} %refs_4_.1, s32[3,32,144]{2,1,0:T(8,128)} %refs_5_.1, ...), custom_call_target="tpu_custom_call" | custom-call | tf_op jit(solution)/shard_map/pallas_call | solution.py:511
  27.9 0.7 %copy.11 = f32[6,3,4,1152]{3,2,1,0:T(4,128)} copy(f32[6,3,4,1152]{3,2,1,0:T(4,128)S(1)} %get-tuple-element.2) | data formatting | bytes 663552
  28.6 0.6 %copy.12 = f32[3,4,1152]{2,1,0:T(4,128)} copy(f32[3,4,1152]{2,1,0:T(4,128)S(1)} %get-tuple-element.3) | data formatting | bytes 110592

commit v4 on v3

--- a/solution.py
+++ b/solution.py
@@ -211,8 +211,6 @@
             )
         )
     ]
-    for c in loads:
-        c.start()
     barrier = pltpu.get_barrier_semaphore()
     for d in range(1, levs):
         pl.semaphore_signal(
@@ -222,6 +220,8 @@
         pl.semaphore_signal(
             barrier, inc=1, device_id={"lat": lax.rem(me + d, lats)}, device_id_type=MESH
         )
+    for c in loads:
+        c.start()
     for c in loads[:3]:
         c.wait()
     for level in range(levels):
@@ -236,6 +236,15 @@
                 pack_c[level, r, g : g + 1, :] = courant[g, r, at, :]
                 pack_c[level, r, g + 2 : g + 3, :] = offsets[g, r, at, :].astype(jnp.float32)
 
+    for c in loads[3:]:
+        c.wait()
+    first = []
+    for p in range(levs):
+        for r in range(rows):
+            lo = p * levels
+            ks = lo + lax.broadcasted_iota(jnp.int32, (levels, piece), 0)
+            rpack[p, 0, r] = (remap_level[r, lo : lo + levels, :] - ks).astype(jnp.float32)
+            rpack[p, 1, r] = remap_weight[r, lo : lo + levels, :]
     pl.semaphore_wait(barrier, lats + levs - 2)
     fwd = [[] for _ in groups]
     for g in range(parts):
@@ -263,15 +272,6 @@
             c.start()
             fwd[g].append(c)
 
-    for c in loads[3:]:
-        c.wait()
-    first = []
-    for p in range(levs):
-        for r in range(rows):
-            lo = p * levels
-            ks = lo + lax.broadcasted_iota(jnp.int32, (levels, piece), 0)
-            rpack[p, 0, r] = (remap_level[r, lo : lo + levels, :] - ks).astype(jnp.float32)
-            rpack[p, 1, r] = remap_weight[r, lo : lo + levels, :]
     for d in range(1, levs):
         peer = lax.rem(lev + d, levs)
         c = remote(rpack.at[peer], rrecv.at[lev], rs.at[d], rr.at[d], "lev", peer)

time: 29.4 us -> 29.4 us (level)
  no operation moved by 1% of the time
where the time goes in v4:
time: 29.4 us; the launch traced here: 29.2 us
  Pallas kernels  27.3 us (93%)
  local copies, waits for them, and re-layouts  1.35 us (5%)
  between operations  0.64 us (2%)
    pallas_call x1, Pallas kernels, fused(): pl.pallas_call(functools.partial(kernel, lats, levs, chunks), out_shape=(...  27.3 us
    unnamed x2, local copies, waits for them, and re-layouts  1.35 us

profile of v4, /device:TPU:0, one launch (start us, length us, event | category | flops | bytes accessed | tf_op | source)
XLA Modules:
  0.0 29.2 jit_solution(11337725855023378785)
XLA Ops:
  0.6 27.3 %shard_map.86 = (f32[6,3,4,1152]{3,2,1,0:T(4,128)S(1)}, f32[3,4,1152]{2,1,0:T(4,128)S(1)}) custom-call(f32[6,3,4,1152]{3,2,1,0:T(4,128)} %refs_0_.1, f32[2,3,4,1152]{3,2,1,0:T(4,128)} %refs_1_.1, s32[2,3,4,1152]{3,2,1,0:T(4,128)} %refs_2_.1, f32[3,4,1152]{2,1,0:T(4,128)} %refs_3_.1, f32[3,1152]{1,0:T(4,128)} %refs_4_.1, s32[3,32,144]{2,1,0:T(8,128)} %refs_5_.1, ...), custom_call_target="tpu_custom_call" | custom-call | tf_op jit(solution)/shard_map/pallas_call | solution.py:511
  27.9 0.7 %copy.11 = f32[6,3,4,1152]{3,2,1,0:T(4,128)} copy(f32[6,3,4,1152]{3,2,1,0:T(4,128)S(1)} %get-tuple-element.2) | data formatting | bytes 663552
  28.6 0.6 %copy.12 = f32[3,4,1152]{2,1,0:T(4,128)} copy(f32[3,4,1152]{2,1,0:T(4,128)S(1)} %get-tuple-element.3) | data formatting | bytes 110592
